TPU v7x, 128 devices: a whole 4x4x4 slice. The times are simulated.
128 devices in a mesh: req: 32 (over y, z, core), tp: 4 (over x).
Axes of the slice: x: 4, y: 4, z: 4, core: 2. Of those that a mesh axis runs over, the one named last changes fastest.
Arguments:
- states: bfloat16 [64, 512, 1024], P('req', 'tp'), may hold values from -45 to 45
- lengths: int32 [64], P('req'), may hold values from 3 to 512, as said below
- w_qkv: bfloat16 [1024, 3, 1024], P(None, None, 'tp'), may hold values from -0.1875 to 0.1875
- b_qkv: float32 [3, 1024], P(None, 'tp'), may hold values from -3 to 3
- w_out: bfloat16 [1024, 1024], P('tp'), may hold values from -0.1875 to 0.1875
- b_out: float32 [1024], replicated, may hold values from -3 to 3
- ln1_gain: float32 [1024], replicated, may hold values from 0.1 to 1.9
- ln1_shift: float32 [1024], replicated, may hold values from -3 to 3
- w_up: bfloat16 [1024, 4096], P(None, 'tp'), may hold values from -0.1875 to 0.1875
- b_up: float32 [4096], P('tp'), may hold values from -3 to 3
- w_down: bfloat16 [4096, 1024], P('tp'), may hold values from -0.09375 to 0.09375
- b_down: float32 [1024], replicated, may hold values from -3 to 3
- ln2_gain: float32 [1024], replicated, may hold values from 0.1 to 1.9
- ln2_shift: float32 [1024], replicated, may hold values from -3 to 3
- index_rows: bfloat16 [524288, 1024], P(('req', 'tp')), may hold values from -0.1875 to 0.1875
- cand_ids: int32 [64, 64], P('req', 'tp'), may hold values from 0 to 524287
Outputs:
- hidden_out: bfloat16 [64, 512, 1024], P('req', 'tp')
- scores: float32 [64, 64], P('req', 'tp')
Inputs may be any that keep to these rules, and one draw needn't show every extreme that they name: Valid positions are the first lengths ones of a text; in every draw some text has 512.
All inputs are finite; a program needn't handle non-finite values.
Results may differ from a plain program's by a relative error of at most 0.015.
Values may be sent and summed in bfloat16 or wider, within the bound.
A program may use at most 128 MiB of HBM per device.

v0:
```python
import jax
import jax.numpy as jnp
from jax import lax
from jax.sharding import PartitionSpec as P

HEAD_DIM = 64
WINDOW = 512
layer_eps = 1e-05
norm_eps = 1e-06


def layer_norm(values, gain, shift):
    centre = values - jnp.mean(values, axis=-1, keepdims=True)
    spread = jnp.mean(centre * centre, axis=-1, keepdims=True)
    return centre * lax.rsqrt(spread + layer_eps) * gain + shift


def window_attention(queries_h, keys_h, values_h, length):
    seq_len = queries_h.shape[0]
    half_window = WINDOW // 2
    padding = ((half_window, half_window), (0, 0), (0, 0))
    keys_padded = jnp.pad(keys_h, padding)
    values_padded = jnp.pad(values_h, padding)
    scale_factor = HEAD_DIM ** (-0.5)

    def one_block(block_idx):
        blk_start = block_idx * WINDOW
        query_pos = blk_start + jnp.arange(WINDOW, dtype=jnp.int32)
        key_pos = blk_start - half_window + jnp.arange(2 * WINDOW, dtype=jnp.int32)
        keep_mask = (
            (jnp.abs(query_pos[:, None] - key_pos[None, :]) <= half_window)
            & (key_pos[None, :] >= 0)
            & (key_pos[None, :] < length)
        )
        logits = (
            jnp.einsum("qhe,khe->hqk", queries_h, keys_padded, preferred_element_type=jnp.float32)
            * scale_factor
        )
        logits = jnp.where(keep_mask[None], logits, jnp.float32(-1e30))
        top_val = jnp.max(logits, axis=-1, keepdims=True)
        expo = jnp.exp(logits - top_val)
        attn_weights = (expo / jnp.sum(expo, axis=-1, keepdims=True)).astype(jnp.bfloat16)
        context = jnp.einsum(
            "hqk,khe->qhe", attn_weights, values_padded, preferred_element_type=jnp.float32
        )
        context = jnp.where((query_pos < length)[:, None, None], context, jnp.float32(0.0))
        return context.astype(jnp.bfloat16)

    blocks = lax.map(one_block, jnp.arange(seq_len // WINDOW, dtype=jnp.int32))
    return blocks.reshape(seq_len, queries_h.shape[1] * HEAD_DIM)


def per_device(
    states,
    lengths,
    w_qkv,
    b_qkv,
    w_out,
    b_out,
    ln1_gain,
    ln1_shift,
    w_up,
    b_up,
    w_down,
    b_down,
    ln2_gain,
    ln2_shift,
    index_rows,
    cand_ids,
):
    tp_count = lax.axis_size("tp")
    tp_rank = lax.axis_index("tp")
    req_count = lax.axis_size("req")
    text_count, row_share, model_width = states.shape
    full_states = lax.all_gather(states, "tp", axis=1, tiled=True)
    seq_len = full_states.shape[1]
    local_width = w_qkv.shape[2]
    heads_here = local_width // HEAD_DIM
    projected = (
        jnp.einsum("tsd,dce->tsce", full_states, w_qkv, preferred_element_type=jnp.float32) + b_qkv
    ).astype(jnp.bfloat16)
    queries_h = projected[:, :, 0].reshape(text_count, seq_len, heads_here, HEAD_DIM)
    keys_h = projected[:, :, 1].reshape(text_count, seq_len, heads_here, HEAD_DIM)
    values_h = projected[:, :, 2].reshape(text_count, seq_len, heads_here, HEAD_DIM)

    def per_text(bundle):
        return window_attention(bundle[0], bundle[1], bundle[2], bundle[3])

    context = lax.map(per_text, (queries_h, keys_h, values_h, lengths))
    partial_value = jnp.einsum("tsk,kd->tsd", context, w_out, preferred_element_type=jnp.float32)
    attn_sum = lax.psum(partial_value.astype(jnp.bfloat16), "tp").astype(jnp.float32)
    normed_full = layer_norm(
        full_states.astype(jnp.float32) + attn_sum + b_out, ln1_gain, ln1_shift
    ).astype(jnp.bfloat16)
    normed_local = lax.dynamic_slice_in_dim(normed_full, tp_rank * row_share, row_share, 1)
    up_act = jax.nn.gelu(
        jnp.einsum("tsd,df->tsf", normed_full, w_up, preferred_element_type=jnp.float32) + b_up,
        approximate=False,
    ).astype(jnp.bfloat16)
    down_part = jnp.einsum("tsf,fd->tsd", up_act, w_down, preferred_element_type=jnp.float32)
    down_sum = lax.psum_scatter(
        down_part.astype(jnp.bfloat16), "tp", scatter_dimension=1, tiled=True
    ).astype(jnp.float32)
    hidden_out = layer_norm(
        normed_local.astype(jnp.float32) + down_sum + b_down, ln2_gain, ln2_shift
    ).astype(jnp.bfloat16)
    positions = tp_rank * row_share + jnp.arange(row_share, dtype=jnp.int32)
    is_valid = positions[None, :] < lengths[:, None]
    local_pool = jnp.sum(
        jnp.where(is_valid[:, :, None], hidden_out.astype(jnp.float32), jnp.float32(0.0)), axis=1
    )
    pooled = lax.psum(local_pool, "tp") / lengths.astype(jnp.float32)[:, None]
    query_vec = (
        pooled * lax.rsqrt(jnp.mean(pooled * pooled, axis=-1, keepdims=True) + norm_eps)
    ).astype(jnp.bfloat16)
    all_queries = lax.all_gather(query_vec, "req", axis=0, tiled=True)
    quarter = cand_ids.shape[1]
    gathered_ids = lax.all_gather(cand_ids, ("req", "tp"), axis=0, tiled=True)
    all_ids = (
        gathered_ids.reshape(req_count, tp_count, text_count, quarter)
        .transpose(0, 2, 1, 3)
        .reshape(req_count * text_count, tp_count * quarter)
    )
    rows_here = index_rows.shape[0]
    first_row = (lax.axis_index("req") * tp_count + tp_rank) * rows_here
    local_ids = all_ids - first_row
    is_owned = (local_ids >= 0) & (local_ids < rows_here)
    safe_ids = jnp.clip(local_ids, 0, rows_here - 1)
    fetched = jnp.take(index_rows, safe_ids.reshape(-1), axis=0).reshape(
        safe_ids.shape[0], safe_ids.shape[1], model_width
    )
    picked = jnp.einsum("td,tcd->tc", all_queries, fetched, preferred_element_type=jnp.float32)
    owner_terms = jnp.where(is_owned, picked, jnp.float32(0.0))
    owner_terms = (
        owner_terms.reshape(req_count, text_count, tp_count, quarter)
        .transpose(0, 2, 1, 3)
        .reshape(req_count * tp_count * text_count, quarter)
    )
    scores = lax.psum_scatter(owner_terms, ("req", "tp"), scatter_dimension=0, tiled=True)
    return (hidden_out, scores)


def solution(mesh):
    placed = (
        P("req", "tp", None),
        P("req"),
        P(None, None, "tp"),
        P(None, "tp"),
        P("tp", None),
        P(),
        P(),
        P(),
        P(None, "tp"),
        P("tp"),
        P("tp", None),
        P(),
        P(),
        P(),
        P(("req", "tp"), None),
        P("req", "tp"),
    )
    return jax.shard_map(
        per_device,
        mesh=mesh,
        in_specs=placed,
        out_specs=(P("req", "tp", None), P("req", "tp")),
        check_vma=False,
    )
```

profile of v0, /device:TPU:1, one launch (start us, length us, event | category | flops | bytes accessed | tf_op | source)
XLA Modules:
  0.0 362.5 jit_solution(10841223569805811967)
XLA Ops:
  7.2 0.7 all-gather.4.cloned.1.call-update
  8.0 35.7 %all-gather.4.cloned.1.call-done = bf16[2,512,1024]{2,1,0:T(8,128)(2,1)} async-done(((bf16[2,128,1024]{2,1,0:T(8,128)(2,1)}), bf16[2,512,1024]{2,1,0:T(8,128)(2,1)}) %all-gather.4.cloned.1.call-update) | async-done | bytes 2097168 | tf_op jit(solution)/shard_map/all_gather | solution.py:75
  43.7 3.9 %add_convert_fusion.1 = bf16[2,512,3,256]{1,3,2,0:T(8,128)(2,1)S(1)} fusion(f32[3,256]{1,0:T(4,128)} %param.21, bf16[1024,3,256]{2,0,1:T(8,128)(2,1)} %param.20, bf16[2,512,1024]{2,1,0:T(8,128)(2,1)} %all-gather.4.cloned.1.call-done), kind=kOutput, calls=%fused_computation.68 | convolution fusion | flops 1612185600 | bytes 5245952 | tf_op jit(solution)/shard_map/tsd,dce->tsce/dot_general | solution.py:80
  47.6 1.2 fusion.150
  48.8 33.0 %while.17 = (s32[]{:T(128)}, bf16[2,512,256]{1,2,0:T(8,128)(2,1)}, s32[2]{0:T(128)S(1)}, bf16[2,512,4,64]{1,3,2,0:T(8,128)(2,1)}, bf16[2,512,4,64]{1,3,2,0:T(8,1...) while((s32[]{:T(128)}, bf16[2,512,256]{1,2,0:T(8,128)(2,1)}, s32[2]{0:T(128)S(1)}, ...), condition=%wide.region_3.4_spmd, body=%wide.region_0.3_spmd.sunk | while | flops 552343040 | bytes 24671904 | solution.py:89
  48.8 0.7 dynamic_slice.64
  49.5 0.7 fusion.164
  50.2 0.7 fusion.165
  50.9 1.1 dynamic-slice_bitcast_fusion.3
  52.0 6.9 %fusion.166 = (f32[4,512]{1,0:T(4,128)S(1)}, f32[4,512,1024]{2,1,0:T(8,128)}) fusion(pred[512,1024]{1,0:T(8,128)(4,1)S(1)} %fusion.165, bf16[512,4,64]{0,2,1:T(8,128)(2,1)S(1)} %get-tuple-element.195, bf16[2,512,4,64]{1,3,2,0:T(8,128)(2,1)} %get-tuple-element.217, s32[]{:T(128)} %get-tuple-element.206), kind=kOutput, calls=%fused_computation.171.clone.1 | convolution fusion | flops 276825088 | bytes 9445888 | tf_op jit(solution)/shard_map/while/body/eval_jaxpr/while/body/eval_jaxpr/sub | solution.py:41
  58.9 0.7 iota_compare_fusion.2
  59.6 4.9 %fusion.167 = bf16[4,64,512]{2,1,0:T(8,128)(2,1)S(1)} fusion(f32[4,512,1024]{2,1,0:T(8,128)} %get-tuple-element.196, f32[4,512]{1,0:T(4,128)S(1)} %get-tuple-element.197, bf16[512,4,64]{0,2,1:T(8,128)(2,1)S(1)} %get-tuple-element.198, pred[512]{0:T(512)(128)(4,1)S(1)} %iota_compare_fusion.2), kind=kOutput, calls=%fused_computation.14.clone.1 | convolution fusion | flops 272891904 | bytes 8921600 | tf_op jit(solution)/shard_map/while/body/eval_jaxpr/while/body/eval_jaxpr/hqk,khe->qhe/dot_general | solution.py:43
  64.5 0.8 copy-done.5
  65.3 0.7 dynamic_slice.64
  66.0 0.7 fusion.164
  66.7 0.7 fusion.165
  67.4 1.1 dynamic-slice_bitcast_fusion.3
  68.5 6.9 %fusion.166 = (f32[4,512]{1,0:T(4,128)S(1)}, f32[4,512,1024]{2,1,0:T(8,128)}) fusion(pred[512,1024]{1,0:T(8,128)(4,1)S(1)} %fusion.165, bf16[512,4,64]{0,2,1:T(8,128)(2,1)S(1)} %get-tuple-element.195, bf16[2,512,4,64]{1,3,2,0:T(8,128)(2,1)} %get-tuple-element.217, s32[]{:T(128)} %get-tuple-element.206), kind=kOutput, calls=%fused_computation.171.clone.1 | convolution fusion | flops 276825088 | bytes 9445888 | tf_op jit(solution)/shard_map/while/body/eval_jaxpr/while/body/eval_jaxpr/sub | solution.py:41
  75.4 0.7 iota_compare_fusion.2
  76.1 4.9 %fusion.167 = bf16[4,64,512]{2,1,0:T(8,128)(2,1)S(1)} fusion(f32[4,512,1024]{2,1,0:T(8,128)} %get-tuple-element.196, f32[4,512]{1,0:T(4,128)S(1)} %get-tuple-element.197, bf16[512,4,64]{0,2,1:T(8,128)(2,1)S(1)} %get-tuple-element.198, pred[512]{0:T(512)(128)(4,1)S(1)} %iota_compare_fusion.2), kind=kOutput, calls=%fused_computation.14.clone.1 | convolution fusion | flops 272891904 | bytes 8921600 | tf_op jit(solution)/shard_map/while/body/eval_jaxpr/while/body/eval_jaxpr/hqk,khe->qhe/dot_general | solution.py:43
  81.0 0.8 copy-done.5
  81.8 3.2 convolution_convert_fusion
  85.1 0.2 reduce-scatter.2.cloned.1.call-start
  85.3 58.6 %all-reduce.5.cloned.1.call-done = bf16[2,512,1024]{2,1,0:T(8,128)(2,1)} async-done(((bf16[2,512,1024]{2,1,0:T(8,128)(2,1)}), bf16[2,512,1024]{2,1,0:T(8,128)(2,1)}) %all-reduce.5.cloned.1.call-update) | async-done | bytes 2097168 | tf_op jit(solution)/shard_map/psum | solution.py:91
  143.9 3.1 fusion.54
  147.1 0.3 copy-done.2
  147.4 1.1 multiply_reduce_fusion
  148.5 1.2 add_convert_fusion
  149.8 3.4 fusion.103
  153.2 12.5 %fusion.92 = bf16[2,512,1024]{2,1,0:T(8,128)(2,1)} fusion(bf16[1024,1024]{1,0:T(8,128)(2,1)S(1)} %copy-done.13, f32[2,512,1024]{2,1,0:T(8,128)S(1)} %get-tuple-element.149, f32[1024]{0:T(1024)S(1)} %copy-done.14, u8[512,1024]{1,0:T(8,128)(4,1)S(1)} %get-tuple-element.123, u8[512,1024]{1,0:T(8,128)(4,1)S(1)} %get-tuple-element.122), kind=kOutput, calls=%fused_computation.105 | convolution fusion | flops 2222981120 | bytes 9441280 | tf_op jit(solution)/shard_map/tsf,fd->tsd/dot_general | solution.py:100
  165.7 55.1 %all-gather = s32[128,2,16]{2,1,0:T(2,128)S(1)} all-gather(s32[1,2,16]{2,1,0:T(2,128)S(1)} %bitcast.89), channel_id=1, replica_groups=mesh['req'=32,'tp'=4] {'req','tp'}, dimensions={0}, use_global_device_ids=true | all-gather | bytes 16512 | tf_op jit(solution)/shard_map/all_gather | solution.py:118
  220.9 0.1 subtract_clamp_fusion
  221.0 0.1 min.24
  221.2 0.1 min.22
  221.3 0.1 compare_and_fusion
  221.5 0.1 and.61
  221.7 25.4 %gather_fusion = bf16[4096,1024]{1,0:T(8,128)(2,1)} fusion(bf16[4096,1024]{1,0:T(8,128)(2,1)} %param.32, s32[4096]{0:T(1024)S(1)} %broadcast_clamp_fusion), kind=kCustom, calls=%fused_computation | custom fusion | bytes 16793600 | tf_op jit(solution)/shard_map/jit(_take)/gather | solution.py:129
  247.2 1.5 fusion.104
  248.6 1.5 multiply_reduce_fusion.1
  250.2 2.4 select_reduce_fusion
  252.6 8.4 %psum.15 = f32[2,1024]{1,0:T(2,128)S(1)} all-reduce(f32[2,1024]{1,0:T(2,128)S(1)} %get-tuple-element.138), channel_id=1, replica_groups=mesh['req'=32,'tp'=4] {'tp'}, use_global_device_ids=true, to_apply=%region_11.12 | all-reduce | flops 2048 | bytes 16384 | tf_op jit(solution)/shard_map/psum | solution.py:112
  261.0 0.2 multiply_reduce_fusion.2
  261.3 25.0 %all-gather.1 = bf16[32,2,1024]{2,1,0:T(2,128)(2,1)S(1)} all-gather(bf16[1,2,1024]{2,1,0:T(2,128)(2,1)S(1)} %fusion.108), channel_id=1, replica_groups=mesh['req'=32,'tp'=4] {'req'}, dimensions={0}, use_global_device_ids=true | all-gather | bytes 135168 | tf_op jit(solution)/shard_map/all_gather | solution.py:116
  286.3 0.1 reshape.275
  286.4 4.7 %fusion.41 = f32[64,1,64]{2,1,0:T(1,128)S(1)} fusion(bf16[64,1024,1]{1,2,0:T(2,128)(2,1)S(1)} %reshape.275, bf16[64,64,1024]{2,1,0:T(8,128)(2,1)} %bitcast.75, pred[64,64]{1,0:T(8,128)(4,1)S(1)} %compare_and_fusion.1), kind=kOutput, calls=%fused_computation.38 | convolution fusion | flops 12582912 | bytes 8540160 | tf_op jit(solution)/shard_map/td,tcd->tc/dot_general | solution.py:132
  291.2 0.1 reshape.240
  291.4 64.0 %all-reduce.2 = f32[256,16]{1,0:T(8,128)S(1)} all-reduce(f32[256,16]{1,0:T(8,128)S(1)} %bitcast.82), channel_id=3, replica_groups=mesh['req'=32,'tp'=4] {'req','tp'}, use_global_device_ids=true, to_apply=%region_13.14.clone | all-reduce | flops 4096 | bytes 32768
  355.4 0.6 constant_dynamic-slice_fusion
  (59 shorter events, 0.7 us)
Async XLA Ops:
  7.2 142.6 %copy-start = (bf16[1024,1024]{1,0:T(8,128)(2,1)S(1)}, bf16[1024,1024]{1,0:T(8,128)(2,1)}, u32[]{:S(2)}) copy-start(bf16[1024,1024]{1,0:T(8,128)(2,1)} %param.26) | copy-start | bytes 6291460
  7.2 36.5 %all-gather.4.cloned.1.call-start = ((), (), s32[]{:S(2)}) async-start(), calls=%async_computation.1 | async-start | bytes 2621440 | tf_op jit(solution)/shard_map/all_gather | solution.py:75
  7.9 136.0 %all-reduce.5.cloned.1.call-start = ((), (), s32[]{:S(2)}) async-start(), calls=%async_computation.2 | async-start | bytes 4194304 | tf_op jit(solution)/shard_map/psum | solution.py:91
  8.0 40.8 %copy-start.15 = (s32[2]{0:T(128)S(1)}, s32[2]{0:T(128)}, u32[]{:S(2)}) copy-start(s32[2]{0:T(128)} %param.19) | copy-start | bytes 28
  59.6 4.9 %copy-start.4 = (bf16[2,512,256]{1,2,0:T(8,128)(2,1)S(1)}, bf16[2,512,256]{1,2,0:T(8,128)(2,1)}, u32[]{:S(2)}) copy-start(bf16[2,512,256]{1,2,0:T(8,128)(2,1)} %get-tuple-element.207) | copy-start | bytes 1572868 | tf_op jit(solution)/shard_map/while
  64.5 0.8 copy-start.5
  76.0 4.9 %copy-start.4 = (bf16[2,512,256]{1,2,0:T(8,128)(2,1)S(1)}, bf16[2,512,256]{1,2,0:T(8,128)(2,1)}, u32[]{:S(2)}) copy-start(bf16[2,512,256]{1,2,0:T(8,128)(2,1)} %get-tuple-element.207) | copy-start | bytes 1572868 | tf_op jit(solution)/shard_map/while
  81.0 0.8 copy-start.5
  81.8 62.1 %copy-start.7 = (f32[1024]{0:T(1024)S(1)}, f32[1024]{0:T(1024)}, u32[]{:S(2)}) copy-start(f32[1024]{0:T(1024)} %param.23) | copy-start | bytes 12292
  85.1 63.4 %copy-start.10 = (f32[1024]{0:T(1024)S(1)}, f32[1024]{0:T(1024)}, u32[]{:S(2)}) copy-start(f32[1024]{0:T(1024)} %param.25) | copy-start | bytes 12292
  85.1 63.4 %copy-start.11 = (f32[1024]{0:T(1024)S(1)}, f32[1024]{0:T(1024)}, u32[]{:S(2)}) copy-start(f32[1024]{0:T(1024)} %param.24) | copy-start | bytes 12292
  85.1 162.1 %reduce-scatter.2.cloned.1.call-start = ((), (), s32[]{:S(2)}) async-start(), calls=%async_computation.3 | async-start | bytes 2621440 | tf_op jit(solution)/shard_map/reduce_scatter | solution.py:101
  143.9 3.1 copy-start.1
  143.9 3.5 copy-start.2
  148.4 1.3 copy-start.14
  149.8 3.4 copy-start.3
  149.8 3.4 copy-start.13
  153.2 12.5 %copy-start.12 = (s32[2,16]{1,0:T(2,128)S(1)}, s32[2,16]{1,0:T(2,128)}, u32[]{:S(2)}) copy-start(s32[2,16]{1,0:T(2,128)} %param.33) | copy-start | bytes 388
  221.6 25.5 %copy-start.6 = (f32[1024]{0:T(1024)S(1)}, f32[1024]{0:T(1024)}, u32[]{:S(2)}) copy-start(f32[1024]{0:T(1024)} %param.29) | copy-start | bytes 12292
  221.7 28.5 %copy-start.8 = (f32[1024]{0:T(1024)S(1)}, f32[1024]{0:T(1024)}, u32[]{:S(2)}) copy-start(f32[1024]{0:T(1024)} %param.31) | copy-start | bytes 12292
  221.7 28.5 %copy-start.9 = (f32[1024]{0:T(1024)S(1)}, f32[1024]{0:T(1024)}, u32[]{:S(2)}) copy-start(f32[1024]{0:T(1024)} %param.30) | copy-start | bytes 12292
Sparse Core Ops, SparseCore 0:
  9.7 34.0 all-gather.3
  85.2 58.6 all-reduce.4
  165.8 29.5 reduce-scatter.1
where the time goes:
time: 363 us
  blocking collectives  153 us (42%)
  waiting for transfers between devices  95 us (26%)
  matrix products  51.4 us (14%)
  local copies, waits for them, and re-layouts  33.3 us (9%)
  other arithmetic  15.6 us (4%)
  between operations  14.1 us (4%)
    unnamed x1, blocking collectives  64 us
    psum x1, waiting for transfers between devices, per_device(): lax.psum(partial_value.astype(jnp.bfloat16), 'tp').astype(jnp.float32)  58.6 us
    all_gather x1, blocking collectives, per_device(): gathered_ids = lax.all_gather(cand_ids, ('req', 'tp'), axis=0, tiled=True)  55.1 us
    all_gather x1, waiting for transfers between devices, per_device(): full_states = lax.all_gather(states, 'tp', axis=1, tiled=True)  35.7 us
    gather x1, local copies, waits for them, and re-layouts, per_device(): jnp.take(index_rows, safe_ids.reshape(-1), axis=0)  25.4 us
    all_gather x1, blocking collectives, per_device(): all_queries = lax.all_gather(query_vec, 'req', axis=0, tiled=True)  25 us
    sub x2, matrix products, one_block(): expo = jnp.exp(logits - top_val)  13.8 us
    dot_general x1, matrix products, per_device(): jnp.einsum('tsf,fd->tsd', up_act, w_down, preferred_element_type=jnp.floa...  12.5 us
  transfers between devices with their start and end apart: 3, of which 2 were waited for; matrix products, arithmetic and copies ran while one was open for 7% of the time, Pallas kernels for 0%

commit v1 on v0

--- a/solution.py
+++ b/solution.py
@@ -2,6 +2,7 @@
 import jax.numpy as jnp
 from jax import lax
 from jax.sharding import PartitionSpec as P
+from jax.lax import all_to_all, axis_size
 
 HEAD_DIM = 64
 WINDOW = 512
@@ -113,7 +114,11 @@
     query_vec = (
         pooled * lax.rsqrt(jnp.mean(pooled * pooled, axis=-1, keepdims=True) + norm_eps)
     ).astype(jnp.bfloat16)
-    all_queries = lax.all_gather(query_vec, "req", axis=0, tiled=True)
+    axis_total = axis_size("req")
+    item_now = tuple((axis_total if hop_no == 0 else 1 for hop_no in range(query_vec.ndim)))
+    all_queries = all_to_all(
+        jnp.tile(query_vec, item_now), "req", split_axis=0, concat_axis=0, tiled=True
+    )
     quarter = cand_ids.shape[1]
     gathered_ids = lax.all_gather(cand_ids, ("req", "tp"), axis=0, tiled=True)
     all_ids = (

time: 363 us -> 352 us (0.970)
  blocking collectives: 153 us -> 127 us
  waiting for transfers between devices: 95 us -> 103 us
  starting transfers between devices: 0.3 us -> 6.52 us
    all_gather x1 -> x0, blocking collectives: 25 us -> none  [per_device(): all_queries = lax.all_gather(query_vec, 'req', axis=0, tiled=True)]
    all_to_all x0 -> x1, waiting for transfers between devices: none -> 7.79 us  [per_device(): all_to_all(jnp.tile(query_vec, item_now), 'req', split_axis=0, concat_axi...]
    all_to_all x0 -> x1, starting transfers between devices: none -> 6.22 us  [per_device(): all_to_all(jnp.tile(query_vec, item_now), 'req', split_axis=0, concat_axi...]
  transfers between devices with their start and end apart: 3 -> 4, of which waited for: 2 -> 3; matrix products, arithmetic and copies ran while one was open for 7% -> 7% of each run, Pallas kernels for 0% -> 0%
where the time goes in v1:
time: 352 us; the launch traced here: 351 us
  blocking collectives  127 us (36%)
  waiting for transfers between devices  103 us (29%)
  matrix products  51.4 us (15%)
  local copies, waits for them, and re-layouts  34.1 us (10%)
  other arithmetic  15.6 us (4%)
  between operations  14.1 us (4%)
  starting transfers between devices  6.52 us (2%)
    unnamed x1, blocking collectives  63 us
    psum x1, waiting for transfers between devices, per_device(): lax.psum(partial_value.astype(jnp.bfloat16), 'tp').astype(jnp.float32)  58.6 us
    all_gather x1, blocking collectives, per_device(): gathered_ids = lax.all_gather(cand_ids, ('req', 'tp'), axis=0, tiled=True)  55.1 us
    all_gather x1, waiting for transfers between devices, per_device(): full_states = lax.all_gather(states, 'tp', axis=1, tiled=True)  35.7 us
    gather x1, local copies, waits for them, and re-layouts, per_device(): jnp.take(index_rows, safe_ids.reshape(-1), axis=0)  25.4 us
    sub x2, matrix products, one_block(): expo = jnp.exp(logits - top_val)  13.8 us
    dot_general x1, matrix products, per_device(): jnp.einsum('tsf,fd->tsd', up_act, w_down, preferred_element_type=jnp.floa...  12.5 us
    dot_general x2, matrix products, one_block(): jnp.einsum('hqk,khe->qhe', attn_weights, values_padded, preferred_element...  9.8 us
  transfers between devices with their start and end apart: 4, of which 3 were waited for; matrix products, arithmetic and copies ran while one was open for 7% of the time, Pallas kernels for 0%

profile of v1, /device:TPU:1, one launch (start us, length us, event | category | flops | bytes accessed | tf_op | source)
XLA Modules:
  0.0 351.2 jit_solution(13242836005155999237)
XLA Ops:
  7.2 0.7 all-gather.3.cloned.1.call-update
  8.0 35.7 %all-gather.3.cloned.1.call-done = bf16[2,512,1024]{2,1,0:T(8,128)(2,1)} async-done(((bf16[2,128,1024]{2,1,0:T(8,128)(2,1)}), bf16[2,512,1024]{2,1,0:T(8,128)(2,1)}) %all-gather.3.cloned.1.call-update) | async-done | bytes 2097168 | tf_op jit(solution)/shard_map/all_gather | solution.py:76
  43.7 3.9 %add_convert_fusion.1 = bf16[2,512,3,256]{1,3,2,0:T(8,128)(2,1)S(1)} fusion(f32[3,256]{1,0:T(4,128)} %param.21, bf16[1024,3,256]{2,0,1:T(8,128)(2,1)} %param.20, bf16[2,512,1024]{2,1,0:T(8,128)(2,1)} %all-gather.3.cloned.1.call-done), kind=kOutput, calls=%fused_computation.68 | convolution fusion | flops 1612185600 | bytes 5245952 | tf_op jit(solution)/shard_map/tsd,dce->tsce/dot_general | solution.py:81
  47.6 1.2 fusion.149
  48.8 33.0 %while.17 = (s32[]{:T(128)}, bf16[2,512,256]{1,2,0:T(8,128)(2,1)}, s32[2]{0:T(128)S(1)}, bf16[2,512,4,64]{1,3,2,0:T(8,128)(2,1)}, bf16[2,512,4,64]{1,3,2,0:T(8,1...) while((s32[]{:T(128)}, bf16[2,512,256]{1,2,0:T(8,128)(2,1)}, s32[2]{0:T(128)S(1)}, ...), condition=%wide.region_3.4_spmd, body=%wide.region_0.3_spmd.sunk | while | flops 552343040 | bytes 24671904 | solution.py:90
  48.8 0.7 dynamic_slice.64
  49.5 0.7 fusion.163
  50.2 0.7 fusion.164
  50.9 1.1 dynamic-slice_bitcast_fusion.3
  52.0 6.9 %fusion.165 = (f32[4,512]{1,0:T(4,128)S(1)}, f32[4,512,1024]{2,1,0:T(8,128)}) fusion(pred[512,1024]{1,0:T(8,128)(4,1)S(1)} %fusion.164, bf16[512,4,64]{0,2,1:T(8,128)(2,1)S(1)} %get-tuple-element.195, bf16[2,512,4,64]{1,3,2,0:T(8,128)(2,1)} %get-tuple-element.217, s32[]{:T(128)} %get-tuple-element.206), kind=kOutput, calls=%fused_computation.170.clone.1 | convolution fusion | flops 276825088 | bytes 9445888 | tf_op jit(solution)/shard_map/while/body/eval_jaxpr/while/body/eval_jaxpr/sub | solution.py:42
  58.9 0.7 iota_compare_fusion.2
  59.6 4.9 %fusion.166 = bf16[4,64,512]{2,1,0:T(8,128)(2,1)S(1)} fusion(f32[4,512,1024]{2,1,0:T(8,128)} %get-tuple-element.196, f32[4,512]{1,0:T(4,128)S(1)} %get-tuple-element.197, bf16[512,4,64]{0,2,1:T(8,128)(2,1)S(1)} %get-tuple-element.198, pred[512]{0:T(512)(128)(4,1)S(1)} %iota_compare_fusion.2), kind=kOutput, calls=%fused_computation.14.clone.1 | convolution fusion | flops 272891904 | bytes 8921600 | tf_op jit(solution)/shard_map/while/body/eval_jaxpr/while/body/eval_jaxpr/hqk,khe->qhe/dot_general | solution.py:44
  64.5 0.8 copy-done.5
  65.3 0.7 dynamic_slice.64
  66.0 0.7 fusion.163
  66.7 0.7 fusion.164
  67.4 1.1 dynamic-slice_bitcast_fusion.3
  68.5 6.9 %fusion.165 = (f32[4,512]{1,0:T(4,128)S(1)}, f32[4,512,1024]{2,1,0:T(8,128)}) fusion(pred[512,1024]{1,0:T(8,128)(4,1)S(1)} %fusion.164, bf16[512,4,64]{0,2,1:T(8,128)(2,1)S(1)} %get-tuple-element.195, bf16[2,512,4,64]{1,3,2,0:T(8,128)(2,1)} %get-tuple-element.217, s32[]{:T(128)} %get-tuple-element.206), kind=kOutput, calls=%fused_computation.170.clone.1 | convolution fusion | flops 276825088 | bytes 9445888 | tf_op jit(solution)/shard_map/while/body/eval_jaxpr/while/body/eval_jaxpr/sub | solution.py:42
  75.4 0.7 iota_compare_fusion.2
  76.1 4.9 %fusion.166 = bf16[4,64,512]{2,1,0:T(8,128)(2,1)S(1)} fusion(f32[4,512,1024]{2,1,0:T(8,128)} %get-tuple-element.196, f32[4,512]{1,0:T(4,128)S(1)} %get-tuple-element.197, bf16[512,4,64]{0,2,1:T(8,128)(2,1)S(1)} %get-tuple-element.198, pred[512]{0:T(512)(128)(4,1)S(1)} %iota_compare_fusion.2), kind=kOutput, calls=%fused_computation.14.clone.1 | convolution fusion | flops 272891904 | bytes 8921600 | tf_op jit(solution)/shard_map/while/body/eval_jaxpr/while/body/eval_jaxpr/hqk,khe->qhe/dot_general | solution.py:44
  81.0 0.8 copy-done.5
  81.8 3.2 convolution_convert_fusion
  85.1 0.2 reduce-scatter.2.cloned.1.call-start
  85.3 58.6 %all-reduce.5.cloned.1.call-done = bf16[2,512,1024]{2,1,0:T(8,128)(2,1)} async-done(((bf16[2,512,1024]{2,1,0:T(8,128)(2,1)}), bf16[2,512,1024]{2,1,0:T(8,128)(2,1)}) %all-reduce.5.cloned.1.call-update) | async-done | bytes 2097168 | tf_op jit(solution)/shard_map/psum | solution.py:92
  143.9 3.1 fusion.54
  147.1 0.3 copy-done.2
  147.4 1.1 multiply_reduce_fusion
  148.5 1.2 add_convert_fusion
  149.8 3.4 fusion.103
  153.2 12.5 %fusion.92 = bf16[2,512,1024]{2,1,0:T(8,128)(2,1)} fusion(bf16[1024,1024]{1,0:T(8,128)(2,1)S(1)} %copy-done.13, f32[2,512,1024]{2,1,0:T(8,128)S(1)} %get-tuple-element.149, f32[1024]{0:T(1024)S(1)} %copy-done.14, u8[512,1024]{1,0:T(8,128)(4,1)S(1)} %get-tuple-element.123, u8[512,1024]{1,0:T(8,128)(4,1)S(1)} %get-tuple-element.122), kind=kOutput, calls=%fused_computation.105 | convolution fusion | flops 2222981120 | bytes 9441280 | tf_op jit(solution)/shard_map/tsf,fd->tsd/dot_general | solution.py:101
  165.7 55.1 %all-gather = s32[128,2,16]{2,1,0:T(2,128)S(1)} all-gather(s32[1,2,16]{2,1,0:T(2,128)S(1)} %bitcast.87), channel_id=1, replica_groups=mesh['req'=32,'tp'=4] {'req','tp'}, dimensions={0}, use_global_device_ids=true | all-gather | bytes 16512 | tf_op jit(solution)/shard_map/all_gather | solution.py:123
  221.0 0.1 min.24
  221.2 0.1 min.22
  221.3 0.1 compare_and_fusion
  221.5 0.1 and.61
  221.7 25.4 %gather_fusion = bf16[4096,1024]{1,0:T(8,128)(2,1)} fusion(bf16[4096,1024]{1,0:T(8,128)(2,1)} %param.32, s32[4096]{0:T(1024)S(1)} %broadcast_clamp_fusion), kind=kCustom, calls=%fused_computation | custom fusion | bytes 16793600 | tf_op jit(solution)/shard_map/jit(_take)/gather | solution.py:134
  247.1 1.4 fusion.104
  248.6 1.5 multiply_reduce_fusion.1
  250.1 2.4 select_reduce_fusion
  252.5 8.4 %psum.15 = f32[2,1024]{1,0:T(2,128)S(1)} all-reduce(f32[2,1024]{1,0:T(2,128)S(1)} %get-tuple-element.138), channel_id=1, replica_groups=mesh['req'=32,'tp'=4] {'tp'}, use_global_device_ids=true, to_apply=%region_11.12 | all-reduce | flops 2048 | bytes 16384 | tf_op jit(solution)/shard_map/psum | solution.py:113
  261.0 0.2 multiply_reduce_fusion.2
  261.3 0.7 tile.2
  262.0 6.2 %all-to-all-start = ((bf16[32,2,1024]{2,1,0:T(2,128)(2,1)}), bf16[32,2,1024]{2,1,0:T(2,128)(2,1)S(1)}, u32[]{:S(2)}, u32[]{:S(2)}) async-start(bf16[32,2,1024]{2,1,0:T(2,128)(2,1)} %tile.2), calls=%async_computation.1 | async-start | bytes 262144 | tf_op jit(solution)/shard_map/all_to_all | solution.py:119
  268.3 7.8 %all-to-all-done = bf16[32,2,1024]{2,1,0:T(2,128)(2,1)S(1)} async-done(((bf16[32,2,1024]{2,1,0:T(2,128)(2,1)}), bf16[32,2,1024]{2,1,0:T(2,128)(2,1)S(1)}, u32[]{:S(2)}, u32[]{:S(2)}) %all-to-all-start) | async-done | bytes 131104 | tf_op jit(solution)/shard_map/all_to_all | solution.py:119
  276.1 4.7 %fusion.41 = f32[64,1,64]{2,1,0:T(1,128)S(1)} fusion(bf16[64,1024,1]{1,2,0:T(2,128)(2,1)S(1)} %reshape.280, bf16[64,64,1024]{2,1,0:T(8,128)(2,1)} %bitcast.73, pred[64,64]{1,0:T(8,128)(4,1)S(1)} %compare_and_fusion.1), kind=kOutput, calls=%fused_computation.38 | convolution fusion | flops 12582912 | bytes 8540160 | tf_op jit(solution)/shard_map/td,tcd->tc/dot_general | solution.py:137
  280.9 0.1 reshape.247
  281.1 63.0 %all-reduce.2 = f32[256,16]{1,0:T(8,128)S(1)} all-reduce(f32[256,16]{1,0:T(8,128)S(1)} %bitcast.80), channel_id=3, replica_groups=mesh['req'=32,'tp'=4] {'req','tp'}, use_global_device_ids=true, to_apply=%region_13.14.clone | all-reduce | flops 4096 | bytes 32768
  344.1 0.6 constant_dynamic-slice_fusion
  (61 shorter events, 0.8 us)
Async XLA Ops:
  7.2 142.6 %copy-start = (bf16[1024,1024]{1,0:T(8,128)(2,1)S(1)}, bf16[1024,1024]{1,0:T(8,128)(2,1)}, u32[]{:S(2)}) copy-start(bf16[1024,1024]{1,0:T(8,128)(2,1)} %param.26) | copy-start | bytes 6291460
  7.2 36.5 %all-gather.3.cloned.1.call-start = ((), (), s32[]{:S(2)}) async-start(), calls=%async_computation.2 | async-start | bytes 2621440 | tf_op jit(solution)/shard_map/all_gather | solution.py:76
  7.9 136.0 %all-reduce.5.cloned.1.call-start = ((), (), s32[]{:S(2)}) async-start(), calls=%async_computation.3 | async-start | bytes 4194304 | tf_op jit(solution)/shard_map/psum | solution.py:92
  8.0 40.8 %copy-start.15 = (s32[2]{0:T(128)S(1)}, s32[2]{0:T(128)}, u32[]{:S(2)}) copy-start(s32[2]{0:T(128)} %param.19) | copy-start | bytes 28
  59.6 4.9 %copy-start.4 = (bf16[2,512,256]{1,2,0:T(8,128)(2,1)S(1)}, bf16[2,512,256]{1,2,0:T(8,128)(2,1)}, u32[]{:S(2)}) copy-start(bf16[2,512,256]{1,2,0:T(8,128)(2,1)} %get-tuple-element.207) | copy-start | bytes 1572868 | tf_op jit(solution)/shard_map/while
  64.5 0.8 copy-start.5
  76.0 4.9 %copy-start.4 = (bf16[2,512,256]{1,2,0:T(8,128)(2,1)S(1)}, bf16[2,512,256]{1,2,0:T(8,128)(2,1)}, u32[]{:S(2)}) copy-start(bf16[2,512,256]{1,2,0:T(8,128)(2,1)} %get-tuple-element.207) | copy-start | bytes 1572868 | tf_op jit(solution)/shard_map/while
  81.0 0.8 copy-start.5
  81.8 62.1 %copy-start.7 = (f32[1024]{0:T(1024)S(1)}, f32[1024]{0:T(1024)}, u32[]{:S(2)}) copy-start(f32[1024]{0:T(1024)} %param.23) | copy-start | bytes 12292
  85.1 63.4 %copy-start.10 = (f32[1024]{0:T(1024)S(1)}, f32[1024]{0:T(1024)}, u32[]{:S(2)}) copy-start(f32[1024]{0:T(1024)} %param.25) | copy-start | bytes 12292
  85.1 63.4 %copy-start.11 = (f32[1024]{0:T(1024)S(1)}, f32[1024]{0:T(1024)}, u32[]{:S(2)}) copy-start(f32[1024]{0:T(1024)} %param.24) | copy-start | bytes 12292
  85.1 162.0 %reduce-scatter.2.cloned.1.call-start = ((), (), s32[]{:S(2)}) async-start(), calls=%async_computation.4 | async-start | bytes 2621440 | tf_op jit(solution)/shard_map/reduce_scatter | solution.py:102
  143.9 3.1 copy-start.1
  143.9 3.5 copy-start.2
  148.4 1.3 copy-start.14
  149.8 3.4 copy-start.3
  149.8 3.4 copy-start.13
  153.2 12.5 %copy-start.12 = (s32[2,16]{1,0:T(2,128)S(1)}, s32[2,16]{1,0:T(2,128)}, u32[]{:S(2)}) copy-start(s32[2,16]{1,0:T(2,128)} %param.33) | copy-start | bytes 388
  221.6 25.5 %copy-start.6 = (f32[1024]{0:T(1024)S(1)}, f32[1024]{0:T(1024)}, u32[]{:S(2)}) copy-start(f32[1024]{0:T(1024)} %param.29) | copy-start | bytes 12292
  221.7 28.5 %copy-start.8 = (f32[1024]{0:T(1024)S(1)}, f32[1024]{0:T(1024)}, u32[]{:S(2)}) copy-start(f32[1024]{0:T(1024)} %param.31) | copy-start | bytes 12292
  221.7 28.5 %copy-start.9 = (f32[1024]{0:T(1024)S(1)}, f32[1024]{0:T(1024)}, u32[]{:S(2)}) copy-start(f32[1024]{0:T(1024)} %param.30) | copy-start | bytes 12292
  262.0 14.0 %all-to-all-start = ((bf16[32,2,1024]{2,1,0:T(2,128)(2,1)}), bf16[32,2,1024]{2,1,0:T(2,128)(2,1)S(1)}, u32[]{:S(2)}, u32[]{:S(2)}) async-start(bf16[32,2,1024]{2,1,0:T(2,128)(2,1)} %tile.2), calls=%async_computation.1 | async-start | bytes 262144 | tf_op jit(solution)/shard_map/all_to_all | solution.py:119
Sparse Core Ops, SparseCore 0:
  9.7 34.0 all-gather.2
  85.2 58.6 all-reduce.4
  165.8 29.5 reduce-scatter.1
